TPU v7x, 32 devices: a whole 2x2x4 slice. The times are simulated.
32 devices in a mesh: grp: 4 (over x, core), dp: 8 (over z, y).
Axes of the slice: x: 2, y: 2, z: 4, core: 2. Of those that a mesh axis runs over, the one named last changes fastest.
Arguments:
- query: bfloat16 [8, 512, 2560], P('dp', 'grp'), may hold values from -30 to 30
- resp_kv: bfloat16 [8, 512, 1024], P('dp', 'grp'), may hold values from -6 to 6
- prefix_kv: bfloat16 [8, 64, 1024], P('dp', 'grp'), may hold values from -30 to 30
- query_bias: float32 [2560], replicated, may hold values from -3 to 3
- kv_bias: float32 [1024], replicated, may hold values from -3 to 3
- out_grad: bfloat16 [8, 512, 2560], P('dp', 'grp'), may hold values from -6 to 6
- lengths: int32 [8, 4], P('dp', 'grp'), may hold values from 32 to 128
Outputs:
- attended: bfloat16 [8, 512, 2560], P('dp', 'grp')
- query_grad: bfloat16 [8, 512, 2560], P('dp', 'grp')
- resp_kv_grad: bfloat16 [8, 512, 1024], P('dp', 'grp')
- prefix_kv_grad: bfloat16 [8, 64, 1024], P('dp', 'grp')
- query_bias_grad: float32 [2560], replicated
- kv_bias_grad: float32 [1024], replicated
All inputs are finite; a program needn't handle non-finite values.
Results may differ from a plain program's by a relative error of at most 0.013.
The roundings to bfloat16 on the way count: a program that leaves them out, or rounds other values in their place, can miss the bound.
Values may be sent and summed in bfloat16 or wider, within the bound.
A program may use at most 64 MiB of HBM per device.

v0:
```python
import jax
import jax.numpy as jnp
from jax import lax
from jax.sharding import PartitionSpec as P

QH = 20
KVH = 4
HD = 128
NEG_BIG = -1e30


def attend_group(queries, cotangent, key_blocks, value_blocks, allows):
    factor = queries.shape[-1] ** (-0.5)
    scores = []
    for keys, allow in zip(key_blocks, allows):
        raw = jnp.einsum("thd,sd->hts", queries, keys, preferred_element_type=jnp.float32) * factor
        scores.append(jnp.where(allow[None], raw, NEG_BIG))
    highest = jnp.max(scores[0], -1, keepdims=True)
    for item in scores[1:]:
        highest = jnp.maximum(highest, jnp.max(item, -1, keepdims=True))
    powers = [jnp.exp(item - highest) for item in scores]
    totals = sum((jnp.sum(item, -1, keepdims=True) for item in powers))
    chances = [item / totals for item in powers]
    rounded = [item.astype(jnp.bfloat16) for item in chances]
    output = sum(
        (
            jnp.einsum("hts,sd->thd", wts, vals, preferred_element_type=jnp.float32)
            for wts, vals in zip(rounded, value_blocks)
        )
    )
    slopes = [
        jnp.einsum("thd,sd->hts", cotangent, vals, preferred_element_type=jnp.float32)
        for vals in value_blocks
    ]
    row_dot = sum(
        (jnp.sum(prob * slope, -1, keepdims=True) for prob, slope in zip(chances, slopes))
    )
    shifted = [
        (prob * (slope - row_dot)).astype(jnp.bfloat16) for prob, slope in zip(chances, slopes)
    ]
    query_grad = (
        sum(
            (
                jnp.einsum("hts,sd->thd", dsb, keys, preferred_element_type=jnp.float32)
                for dsb, keys in zip(shifted, key_blocks)
            )
        )
        * factor
    )
    key_grads = [
        jnp.einsum("hts,thd->sd", dsb, queries, preferred_element_type=jnp.float32) * factor
        for dsb in shifted
    ]
    value_grads = [
        jnp.einsum("hts,thd->sd", wts, cotangent, preferred_element_type=jnp.float32)
        for wts in rounded
    ]
    return (output, query_grad, key_grads, value_grads, shifted, rounded)


def local(query, resp_kv, prefix_kv, query_bias, kv_bias, out_grad, lengths):
    group = QH // KVH
    width = KVH * HD
    factor = HD ** (-0.5)
    prefix_own = (prefix_kv[0].astype(jnp.float32) + kv_bias).astype(jnp.bfloat16)
    own_rows = prefix_own.shape[0]
    prefix = lax.all_gather(prefix_own, "grp", axis=0, tiled=True)
    slots = query.shape[1]
    pre_rows = prefix.shape[0]
    length = lengths[0, 0]
    biased_query = (query[0].astype(jnp.float32) + query_bias).astype(jnp.bfloat16)
    own_kv = (resp_kv[0].astype(jnp.float32) + kv_bias).astype(jnp.bfloat16)
    position = jnp.arange(slots, dtype=jnp.int32)
    live = position < length
    grad_live = jnp.where(live[:, None], out_grad[0], jnp.zeros_like(out_grad[0]))
    allow_own = position[None, :] <= position[:, None]
    allow_pre = jnp.ones((slots, pre_rows), dtype=bool)
    queries = biased_query.reshape(slots, KVH, group, HD).transpose(1, 0, 2, 3)
    grads = grad_live.reshape(slots, KVH, group, HD).transpose(1, 0, 2, 3)
    pre_keys = prefix[:, :width].reshape(pre_rows, KVH, HD).transpose(1, 0, 2)
    pre_vals = prefix[:, width:].reshape(pre_rows, KVH, HD).transpose(1, 0, 2)
    own_keys = own_kv[:, :width].reshape(slots, KVH, HD).transpose(1, 0, 2)
    own_vals = own_kv[:, width:].reshape(slots, KVH, HD).transpose(1, 0, 2)

    def per_group(pieces):
        qpart, gpart, pkey, pval, okey, oval = pieces
        output, qgrad, kgrads, vgrads, shifted, rounded = attend_group(
            qpart,
            gpart,
            [jnp.concatenate([pkey, okey], 0)],
            [jnp.concatenate([pval, oval], 0)],
            [jnp.concatenate([allow_pre, allow_own], 1)],
        )
        return (
            output,
            qgrad,
            kgrads[0][:pre_rows],
            vgrads[0][:pre_rows],
            kgrads[0][pre_rows:],
            vgrads[0][pre_rows:],
            shifted[0][:, :, :pre_rows],
            rounded[0][:, :, :pre_rows],
        )

    output, qgrad, pk_grad, pv_grad, ok_grad, ov_grad, pre_shift, pre_prob = lax.map(
        per_group, (queries, grads, pre_keys, pre_vals, own_keys, own_vals)
    )
    output = output.transpose(1, 0, 2, 3).reshape(slots, QH * HD)
    attended = jnp.where(live[:, None], output, 0.0).astype(jnp.bfloat16)
    qgrad = qgrad.transpose(1, 0, 2, 3).reshape(slots, QH * HD)
    own_grad = jnp.concatenate(
        [
            ok_grad.transpose(1, 0, 2).reshape(slots, width),
            ov_grad.transpose(1, 0, 2).reshape(slots, width),
        ],
        -1,
    )
    shift_sum = jnp.sum(pre_shift.astype(jnp.float32), -1)
    prob_sum = jnp.sum(pre_prob.astype(jnp.float32), -1)
    key_total = jnp.einsum("jht,jthd->jd", shift_sum, queries.astype(jnp.float32)) * factor
    value_total = jnp.einsum("jht,jthd->jd", prob_sum, grads.astype(jnp.float32))
    pre_total = jnp.concatenate([key_total.reshape(width), value_total.reshape(width)], -1)
    count = lax.axis_size("grp") * own_rows
    shift_part = lax.slice_in_dim(pre_shift, 0, count, axis=3)
    prob_part = lax.slice_in_dim(pre_prob, 0, count, axis=3)
    key_part = (
        jnp.einsum("jhts,jthd->sjd", shift_part, queries, preferred_element_type=jnp.float32)
        * factor
    )
    value_part = jnp.einsum("jhts,jthd->sjd", prob_part, grads, preferred_element_type=jnp.float32)
    prefix_grad = lax.psum_scatter(
        jnp.concatenate(
            [key_part.reshape(count, width), value_part.reshape(count, width)], -1
        ).astype(jnp.bfloat16),
        "grp",
        scatter_dimension=0,
        tiled=True,
    )
    qsum, kvsum = lax.psum((jnp.sum(qgrad, 0), jnp.sum(own_grad, 0) + pre_total), ("grp", "dp"))
    return (
        attended[None],
        qgrad.astype(jnp.bfloat16)[None],
        own_grad.astype(jnp.bfloat16)[None],
        prefix_grad[None],
        qsum,
        kvsum,
    )


def solution(mesh):
    return jax.shard_map(
        local,
        mesh=mesh,
        in_specs=(
            P("dp", "grp", None),
            P("dp", "grp", None),
            P("dp", "grp", None),
            P(),
            P(),
            P("dp", "grp", None),
            P("dp", "grp"),
        ),
        out_specs=(
            P("dp", "grp", None),
            P("dp", "grp", None),
            P("dp", "grp", None),
            P("dp", "grp", None),
            P(),
            P(),
        ),
        check_vma=False,
    )
```

profile of v0, /device:TPU:0, one launch (start us, length us, event | category | flops | bytes accessed | tf_op | source)
XLA Modules:
  0.0 98.3 jit_solution(17740030026731421601)
XLA Ops:
  8.0 0.8 add.43
  8.7 0.8 fusion.49
  9.5 6.5 %all_gather.3 = bf16[64,1024]{1,0:T(8,128)(2,1)S(1)} all-gather(bf16[16,1024]{1,0:T(8,128)(2,1)S(1)} %fusion.49), channel_id=1, replica_groups=mesh['grp'=4,'dp'=8] {'grp'}, dimensions={0}, use_global_device_ids=true | all-gather | bytes 163840 | tf_op jit(solution)/shard_map/all_gather | solution.py:67
  16.7 1.1 %copy.17 = bf16[1,128,1024]{1,2,0:T(8,128)(2,1)S(1)} copy(bf16[1,128,1024]{2,1,0:T(8,128)(2,1)} %param.10) | data formatting | bytes 524288 | tf_op args[1]
  18.1 0.7 fusion.57
  20.0 22.9 %while.21 = (s32[]{:T(128)}, bf16[4,128,5,128]{1,3,2,0:T(8,128)(2,1)}, f32[4,128,5,128]{1,3,2,0:T(8,128)}, f32[4,128,128]{1,2,0:T(8,128)}, f32[4,128,128]{1,2,0:...) while((s32[]{:T(128)}, ...), condition=%wide.region_4.5_spmd.clone, body=%wide.region_0.4_spmd.clone.sunk | while | flops 190725696 | bytes 7174342 | solution.py:105
  20.0 0.7 dynamic-slice_bitcast_fusion.5
  20.9 0.8 constant_dynamic-slice_fusion.5
  23.2 0.6 constant_dynamic-update-slice_fusion.3
  23.9 0.9 fusion.89
  24.8 1.0 fusion.90
  25.7 0.7 dynamic-slice_bitcast_fusion.5
  26.6 0.8 constant_dynamic-slice_fusion.5
  28.9 0.6 constant_dynamic-update-slice_fusion.3
  29.6 0.9 fusion.89
  30.5 1.0 fusion.90
  31.5 0.7 dynamic-slice_bitcast_fusion.5
  32.3 0.8 constant_dynamic-slice_fusion.5
  34.6 0.6 constant_dynamic-update-slice_fusion.3
  35.3 0.9 fusion.89
  36.2 1.0 fusion.90
  37.2 0.7 dynamic-slice_bitcast_fusion.5
  38.1 0.8 constant_dynamic-slice_fusion.5
  40.3 0.6 constant_dynamic-update-slice_fusion.3
  41.0 0.9 fusion.89
  41.9 1.0 fusion.90
  43.7 0.7 pad_maximum_fusion.1
  45.0 0.8 copy-done.2
  46.3 1.1 %copy.34 = bf16[1,128,2560]{2,1,0:T(8,128)(2,1)} copy(bf16[1,128,2560]{1,2,0:T(8,128)(2,1)S(1)} %select_convert_fusion) | data formatting | bytes 1310720
  47.4 1.1 %copy.35 = bf16[1,128,2560]{2,1,0:T(8,128)(2,1)} copy(bf16[1,128,2560]{1,2,0:T(8,128)(2,1)S(1)} %bitcast.229) | data formatting | bytes 1310720
  49.7 41.1 %all-reduce.1 = (f32[2560]{0:T(1024)}, f32[1024]{0:T(1024)}) all-reduce(f32[2560]{0:T(1024)S(1)} %reduce_sum.57, f32[1024]{0:T(1024)S(1)} %maximum_add_fusion), channel_id=1, replica_groups=mesh['grp'=4,'dp'=8] {'grp','dp'}, use_global_device_ids=true, to_apply=%region_7.8 | all-reduce | flops 3584 | bytes 28672 | tf_op jit(solution)/shard_map/psum | solution.py:139
  90.7 0.7 pad_maximum_fusion
  (124 shorter events, 11.6 us)
Async XLA Ops:
  7.2 10.7 %copy-start.9 = (f32[1024]{0:T(1024)S(1)}, f32[1024]{0:T(1024)}, u32[]{:S(2)}) copy-start(f32[1024]{0:T(1024)} %param.13) | copy-start | bytes 12292
  7.2 84.3 %reduce-scatter.2.cloned.1.call-start = ((), (), s32[]{:S(2)}) async-start(), calls=%async_computation.1 | async-start | bytes 163840 | tf_op jit(solution)/shard_map/reduce_scatter | solution.py:131
  7.9 12.0 %copy-start.10 = (pred[128]{0:T(512)(128)(4,1)}, pred[128]{0:T(512)(128)(4,1)S(1)}, u32[]{:S(2)}) copy-start(pred[128]{0:T(512)(128)(4,1)S(1)} %iota_compare_fusion.1) | copy-start | bytes 388
  8.0 10.8 %copy-start.6 = (bf16[1,128,2560]{2,1,0:T(8,128)(2,1)S(1)}, bf16[1,128,2560]{2,1,0:T(8,128)(2,1)}, u32[]{:S(2)}) copy-start(bf16[1,128,2560]{2,1,0:T(8,128)(2,1)} %param.9) | copy-start | bytes 1966084
  18.1 1.1 %copy-start.7 = (bf16[1,128,2560]{2,1,0:T(8,128)(2,1)S(1)}, bf16[1,128,2560]{2,1,0:T(8,128)(2,1)}, u32[]{:S(2)}) copy-start(bf16[1,128,2560]{2,1,0:T(8,128)(2,1)} %param.14) | copy-start | bytes 1966084
  42.9 1.5 %copy-start.1 = (bf16[4,5,128,64]{2,3,1,0:T(8,128)(2,1)}, bf16[4,5,128,64]{2,3,1,0:T(8,128)(2,1)S(1)}, u32[]{:S(2)}) copy-start(bf16[4,5,128,64]{2,3,1,0:T(8,128)(2,1)S(1)} %get-tuple-element.88) | copy-start | bytes 983044
  42.9 1.5 %copy-start.3 = (bf16[4,5,128,64]{2,3,1,0:T(8,128)(2,1)}, bf16[4,5,128,64]{2,3,1,0:T(8,128)(2,1)S(1)}, u32[]{:S(2)}) copy-start(bf16[4,5,128,64]{2,3,1,0:T(8,128)(2,1)S(1)} %get-tuple-element.87) | copy-start | bytes 983044
  42.9 1.6 %copy-start = (f32[4,128,5,128]{1,3,2,0:T(8,128)S(1)}, f32[4,128,5,128]{1,3,2,0:T(8,128)}, u32[]{:S(2)}) copy-start(f32[4,128,5,128]{1,3,2,0:T(8,128)} %get-tuple-element.84) | copy-start | bytes 3932164
  44.9 1.0 copy-start.2
  44.9 1.1 %copy-start.4 = (bf16[4,5,128,64]{2,3,1,0:T(8,128)(2,1)S(1)}, bf16[4,5,128,64]{2,3,1,0:T(8,128)(2,1)}, u32[]{:S(2)}) copy-start(bf16[4,5,128,64]{2,3,1,0:T(8,128)(2,1)} %copy-done.3) | copy-start | bytes 983044
  44.9 1.3 %copy-start.8 = (bf16[4,128,5,128]{1,3,2,0:T(8,128)(2,1)S(1)}, bf16[4,128,5,128]{1,3,2,0:T(8,128)(2,1)}, u32[]{:S(2)}) copy-start(bf16[4,128,5,128]{1,3,2,0:T(8,128)(2,1)} %get-tuple-element.83) | copy-start | bytes 1966084
  44.9 1.3 %copy-start.11 = (pred[128]{0:T(512)(128)(4,1)S(1)}, pred[128]{0:T(512)(128)(4,1)}, u32[]{:S(2)}) copy-start(pred[128]{0:T(512)(128)(4,1)} %copy-done.10) | copy-start | bytes 388
  47.4 1.7 %copy-start.5 = (f32[4,128,128]{1,2,0:T(8,128)S(1)}, f32[4,128,128]{1,2,0:T(8,128)}, u32[]{:S(2)}) copy-start(f32[4,128,128]{1,2,0:T(8,128)} %get-tuple-element.85) | copy-start | bytes 786436
Sparse Core Ops, SparseCore 0:
  44.5 21.3 reduce-scatter.1
where the time goes:
time: 99.2 us; the launch traced here: 98.3 us
  blocking collectives  47.6 us (48%)
  local copies, waits for them, and re-layouts  17.9 us (18%)
  between operations  15 us (15%)
  matrix products  13 us (13%)
  other arithmetic  4.4 us (4%)
    psum x1, blocking collectives, local(): lax.psum((jnp.sum(qgrad, 0), jnp.sum(own_grad, 0) + pre_total), ('grp', '...  41.1 us
    all_gather x1, blocking collectives, local(): prefix = lax.all_gather(prefix_own, 'grp', axis=0, tiled=True)  6.51 us
    unnamed x31, local copies, waits for them, and re-layouts  5.78 us
    dynamic_slice x16, local copies, waits for them, and re-layouts, local(): lax.map(per_group, (queries, grads, pre_keys, pre_vals, own_keys, own_vals))  4.02 us
    dot_general x4, matrix products, attend_group(): jnp.einsum('hts,sd->thd', dsb, keys, preferred_element_type=jnp.float32)  3.86 us
    dot_general x4, matrix products, attend_group(): jnp.einsum('hts,sd->thd', wts, vals, preferred_element_type=jnp.float32)  3.6 us
    dynamic_update_slice x16, local copies, waits for them, and re-layouts, local(): lax.map(per_group, (queries, grads, pre_keys, pre_vals, own_keys, own_vals))  3.37 us
    squeeze x8, local copies, waits for them, and re-layouts, local(): lax.map(per_group, (queries, grads, pre_keys, pre_vals, own_keys, own_vals))  2.9 us
  transfers between devices with their start and end apart: 1, of which 0 were waited for; matrix products, arithmetic and copies ran while one was open for 5% of the time, Pallas kernels for 0%

commit v1 on v0

--- a/solution.py
+++ b/solution.py
@@ -7,6 +7,12 @@
 KVH = 4
 HD = 128
 NEG_BIG = -1e30
+
+
+def name_figure_by_axis(array_here, along_axis, shard_axis):
+    for k in (along_axis, shard_axis):
+        array_here = lax.psum(array_here, axis_name=k)
+    return array_here
 
 
 def attend_group(queries, cotangent, key_blocks, value_blocks, allows):
@@ -136,7 +142,9 @@
         scatter_dimension=0,
         tiled=True,
     )
-    qsum, kvsum = lax.psum((jnp.sum(qgrad, 0), jnp.sum(own_grad, 0) + pre_total), ("grp", "dp"))
+    qsum, kvsum = name_figure_by_axis(
+        (jnp.sum(qgrad, 0), jnp.sum(own_grad, 0) + pre_total), "dp", "grp"
+    )
     return (
         attended[None],
         qgrad.astype(jnp.bfloat16)[None],

time: 99.2 us -> 107 us (1.079)
  blocking collectives: 47.6 us -> 55 us
    psum x1 -> x2, blocking collectives: 41.1 us -> 48.5 us  [name_figure_by_axis(): array_here = lax.psum(array_here, axis_name=k)]
where the time goes in v1:
time: 107 us; the launch traced here: 106 us
  blocking collectives  55 us (51%)
  local copies, waits for them, and re-layouts  17.9 us (17%)
  between operations  15 us (14%)
  matrix products  13 us (12%)
  other arithmetic  4.4 us (4%)
    psum x2, blocking collectives, name_figure_by_axis(): array_here = lax.psum(array_here, axis_name=k)  48.5 us
    all_gather x1, blocking collectives, local(): prefix = lax.all_gather(prefix_own, 'grp', axis=0, tiled=True)  6.51 us
    unnamed x31, local copies, waits for them, and re-layouts  5.78 us
    dynamic_slice x16, local copies, waits for them, and re-layouts, local(): lax.map(per_group, (queries, grads, pre_keys, pre_vals, own_keys, own_vals))  4.02 us
    dot_general x4, matrix products, attend_group(): jnp.einsum('hts,sd->thd', dsb, keys, preferred_element_type=jnp.float32)  3.86 us
    dot_general x4, matrix products, attend_group(): jnp.einsum('hts,sd->thd', wts, vals, preferred_element_type=jnp.float32)  3.6 us
    dynamic_update_slice x16, local copies, waits for them, and re-layouts, local(): lax.map(per_group, (queries, grads, pre_keys, pre_vals, own_keys, own_vals))  3.37 us
    squeeze x8, local copies, waits for them, and re-layouts, local(): lax.map(per_group, (queries, grads, pre_keys, pre_vals, own_keys, own_vals))  2.9 us
  transfers between devices with their start and end apart: 1, of which 0 were waited for; matrix products, arithmetic and copies ran while one was open for 5% of the time, Pallas kernels for 0%

profile of v1, /device:TPU:0, one launch (start us, length us, event | category | flops | bytes accessed | tf_op | source)
XLA Modules:
  0.0 105.7 jit_solution(16916503548243414948)
XLA Ops:
  8.0 0.8 add.47
  8.7 0.8 fusion.49
  9.5 6.5 %all_gather.3 = bf16[64,1024]{1,0:T(8,128)(2,1)S(1)} all-gather(bf16[16,1024]{1,0:T(8,128)(2,1)S(1)} %fusion.49), channel_id=1, replica_groups=mesh['grp'=4,'dp'=8] {'grp'}, dimensions={0}, use_global_device_ids=true | all-gather | bytes 163840 | tf_op jit(solution)/shard_map/all_gather | solution.py:73
  16.7 1.1 %copy.17 = bf16[1,128,1024]{1,2,0:T(8,128)(2,1)S(1)} copy(bf16[1,128,1024]{2,1,0:T(8,128)(2,1)} %param.10) | data formatting | bytes 524288 | tf_op args[1]
  18.1 0.7 fusion.57
  20.0 22.9 %while.21 = (s32[]{:T(128)}, bf16[4,128,5,128]{1,3,2,0:T(8,128)(2,1)}, f32[4,128,5,128]{1,3,2,0:T(8,128)}, f32[4,128,128]{1,2,0:T(8,128)}, f32[4,128,128]{1,2,0:...) while((s32[]{:T(128)}, ...), condition=%wide.region_4.5_spmd.clone, body=%wide.region_0.4_spmd.clone.sunk | while | flops 190725696 | bytes 7174342 | solution.py:111
  20.0 0.7 dynamic-slice_bitcast_fusion.5
  20.9 0.8 constant_dynamic-slice_fusion.5
  23.2 0.6 constant_dynamic-update-slice_fusion.3
  23.9 0.9 fusion.89
  24.8 1.0 fusion.90
  25.7 0.7 dynamic-slice_bitcast_fusion.5
  26.6 0.8 constant_dynamic-slice_fusion.5
  28.9 0.6 constant_dynamic-update-slice_fusion.3
  29.6 0.9 fusion.89
  30.5 1.0 fusion.90
  31.5 0.7 dynamic-slice_bitcast_fusion.5
  32.3 0.8 constant_dynamic-slice_fusion.5
  34.6 0.6 constant_dynamic-update-slice_fusion.3
  35.3 0.9 fusion.89
  36.2 1.0 fusion.90
  37.2 0.7 dynamic-slice_bitcast_fusion.5
  38.1 0.8 constant_dynamic-slice_fusion.5
  41.0 0.9 fusion.89
  41.9 1.0 fusion.90
  43.7 0.7 pad_maximum_fusion.1
  45.0 0.8 copy-done.2
  46.3 1.1 %copy.34 = bf16[1,128,2560]{2,1,0:T(8,128)(2,1)} copy(bf16[1,128,2560]{1,2,0:T(8,128)(2,1)S(1)} %select_convert_fusion) | data formatting | bytes 1310720
  47.4 1.1 %copy.35 = bf16[1,128,2560]{2,1,0:T(8,128)(2,1)} copy(bf16[1,128,2560]{1,2,0:T(8,128)(2,1)S(1)} %bitcast.229) | data formatting | bytes 1310720
  49.7 37.8 %all-reduce.1 = (f32[2560]{0:T(1024)S(1)}, f32[1024]{0:T(1024)S(1)}) all-reduce(f32[2560]{0:T(1024)S(1)} %reduce_sum.57, f32[1024]{0:T(1024)S(1)} %maximum_add_fusion), channel_id=1, replica_groups=mesh['grp'=4,'dp'=8] {'dp'}, use_global_device_ids=true, to_apply=%region_7.8 | all-reduce | flops 3584 | bytes 28672 | tf_op jit(solution)/shard_map/psum | solution.py:14
  87.4 10.7 %all-reduce.2 = (f32[2560]{0:T(1024)}, f32[1024]{0:T(1024)}) all-reduce(f32[2560]{0:T(1024)S(1)} %get-tuple-element.162, f32[1024]{0:T(1024)S(1)} %get-tuple-element.163), channel_id=1, replica_groups=mesh['grp'=4,'dp'=8] {'grp'}, use_global_device_ids=true, to_apply=%region_8.9 | all-reduce | flops 3584 | bytes 28672 | tf_op jit(solution)/shard_map/psum | solution.py:14
  98.2 0.7 pad_maximum_fusion
  (125 shorter events, 12.3 us)
Async XLA Ops:
  7.2 10.7 %copy-start.9 = (f32[1024]{0:T(1024)S(1)}, f32[1024]{0:T(1024)}, u32[]{:S(2)}) copy-start(f32[1024]{0:T(1024)} %param.13) | copy-start | bytes 12292
  7.2 91.7 %reduce-scatter.2.cloned.1.call-start = ((), (), s32[]{:S(2)}) async-start(), calls=%async_computation.1 | async-start | bytes 163840 | tf_op jit(solution)/shard_map/reduce_scatter | solution.py:137
  7.9 12.0 %copy-start.10 = (pred[128]{0:T(512)(128)(4,1)}, pred[128]{0:T(512)(128)(4,1)S(1)}, u32[]{:S(2)}) copy-start(pred[128]{0:T(512)(128)(4,1)S(1)} %iota_compare_fusion.1) | copy-start | bytes 388
  8.0 10.8 %copy-start.6 = (bf16[1,128,2560]{2,1,0:T(8,128)(2,1)S(1)}, bf16[1,128,2560]{2,1,0:T(8,128)(2,1)}, u32[]{:S(2)}) copy-start(bf16[1,128,2560]{2,1,0:T(8,128)(2,1)} %param.9) | copy-start | bytes 1966084
  18.1 1.1 %copy-start.7 = (bf16[1,128,2560]{2,1,0:T(8,128)(2,1)S(1)}, bf16[1,128,2560]{2,1,0:T(8,128)(2,1)}, u32[]{:S(2)}) copy-start(bf16[1,128,2560]{2,1,0:T(8,128)(2,1)} %param.14) | copy-start | bytes 1966084
  42.9 1.5 %copy-start.1 = (bf16[4,5,128,64]{2,3,1,0:T(8,128)(2,1)}, bf16[4,5,128,64]{2,3,1,0:T(8,128)(2,1)S(1)}, u32[]{:S(2)}) copy-start(bf16[4,5,128,64]{2,3,1,0:T(8,128)(2,1)S(1)} %get-tuple-element.88) | copy-start | bytes 983044
  42.9 1.5 %copy-start.3 = (bf16[4,5,128,64]{2,3,1,0:T(8,128)(2,1)}, bf16[4,5,128,64]{2,3,1,0:T(8,128)(2,1)S(1)}, u32[]{:S(2)}) copy-start(bf16[4,5,128,64]{2,3,1,0:T(8,128)(2,1)S(1)} %get-tuple-element.87) | copy-start | bytes 983044
  42.9 1.6 %copy-start = (f32[4,128,5,128]{1,3,2,0:T(8,128)S(1)}, f32[4,128,5,128]{1,3,2,0:T(8,128)}, u32[]{:S(2)}) copy-start(f32[4,128,5,128]{1,3,2,0:T(8,128)} %get-tuple-element.84) | copy-start | bytes 3932164
  44.9 1.0 copy-start.2
  44.9 1.1 %copy-start.4 = (bf16[4,5,128,64]{2,3,1,0:T(8,128)(2,1)S(1)}, bf16[4,5,128,64]{2,3,1,0:T(8,128)(2,1)}, u32[]{:S(2)}) copy-start(bf16[4,5,128,64]{2,3,1,0:T(8,128)(2,1)} %copy-done.3) | copy-start | bytes 983044
  44.9 1.3 %copy-start.8 = (bf16[4,128,5,128]{1,3,2,0:T(8,128)(2,1)S(1)}, bf16[4,128,5,128]{1,3,2,0:T(8,128)(2,1)}, u32[]{:S(2)}) copy-start(bf16[4,128,5,128]{1,3,2,0:T(8,128)(2,1)} %get-tuple-element.83) | copy-start | bytes 1966084
  44.9 1.3 %copy-start.11 = (pred[128]{0:T(512)(128)(4,1)S(1)}, pred[128]{0:T(512)(128)(4,1)}, u32[]{:S(2)}) copy-start(pred[128]{0:T(512)(128)(4,1)} %copy-done.10) | copy-start | bytes 388
  47.4 1.7 %copy-start.5 = (f32[4,128,128]{1,2,0:T(8,128)S(1)}, f32[4,128,128]{1,2,0:T(8,128)}, u32[]{:S(2)}) copy-start(f32[4,128,128]{1,2,0:T(8,128)} %get-tuple-element.85) | copy-start | bytes 786436
Sparse Core Ops, SparseCore 0:
  44.5 21.2 reduce-scatter.1
